TPU v7x, 32 devices: a whole 2x2x4 slice. The times are simulated.
32 devices in a mesh: fsdp: 4 (over x, core), context: 4 (over z), tensor: 2 (over y).
Axes of the slice: x: 2, y: 2, z: 4, core: 2. Of those that a mesh axis runs over, the one named last changes fastest.
Arguments:
- block_input: float32 [8192, 768], P(('fsdp', 'context')), may hold values from -18 to 18
- ln1_gain: float32 [768], replicated, may hold values from 0.1 to 1.9
- ln1_shift: float32 [768], replicated, may hold values from -3 to 3
- qkv_weight: float32 [768, 3, 768], P(('fsdp', 'context'), None, 'tensor'), may hold values from -0.21875 to 0.21875
- qkv_bias: float32 [3, 768], P(None, 'tensor'), may hold values from -3 to 3
- feat_query: float32 [12, 64, 64], P('tensor'), may hold values from -1.5 to 1.5
- feat_key: float32 [12, 64, 64], P('tensor'), may hold values from -1.5 to 1.5
- out_weight: float32 [768, 768], P('tensor', ('fsdp', 'context')), may hold values from -3.5 to 3.5
- out_bias: float32 [768], replicated, may hold values from -3 to 3
- ln2_gain: float32 [768], replicated, may hold values from 0.1 to 1.9
- ln2_shift: float32 [768], replicated, may hold values from -3 to 3
- up_weight: float32 [768, 3072], P(('fsdp', 'context'), 'tensor'), may hold values from -0.21875 to 0.21875
- up_bias: float32 [3072], P('tensor'), may hold values from -3 to 3
- down_weight: float32 [3072, 768], P('tensor', ('fsdp', 'context')), may hold values from -0.109375 to 0.109375
- down_bias: float32 [768], replicated, may hold values from -3 to 3
- lengths: int32 [4], replicated, may hold values from 1024 to 2048, as said below
- deal: int32 [128], P(('fsdp', 'context')), may hold values from 0 to 127, as said below
- cotangent: float32 [8192, 768], P(('fsdp', 'context')), may hold values from -6 to 6
Outputs:
- dealt_output: float32 [128, 64, 768], P(('fsdp', 'context'), 'tensor')
- rms: float32 [3], replicated
- grad_input: float32 [8192, 768], P(('fsdp', 'context'))
- grad_ln1_gain: float32 [768], replicated
- grad_ln1_shift: float32 [768], replicated
- grad_qkv_weight: float32 [768, 3, 768], P(('fsdp', 'context'), None, 'tensor')
- grad_qkv_bias: float32 [3, 768], P(None, 'tensor')
- grad_feat_query: float32 [12, 64, 64], P('tensor')
- grad_feat_key: float32 [12, 64, 64], P('tensor')
- grad_out_weight: float32 [768, 768], P('tensor', ('fsdp', 'context'))
- grad_out_bias: float32 [768], replicated
- grad_ln2_gain: float32 [768], replicated
- grad_ln2_shift: float32 [768], replicated
- grad_up_weight: float32 [768, 3072], P(('fsdp', 'context'), 'tensor')
- grad_up_bias: float32 [3072], P('tensor')
- grad_down_weight: float32 [3072, 768], P('tensor', ('fsdp', 'context'))
- grad_down_bias: float32 [768], replicated
Inputs may be any that keep to these rules, and one draw needn't show every extreme that they name: Sequence lengths; the 4 lengths sum to exactly 8160, and the last of them is exactly 2048. deal is a permutation of the 128 groups. Group j of the device with fsdp index f and context index e (groups numbered along fsdp, then context, then position) goes to position (f * 4 + d) * 8 + e * 2 + r, where the 8 groups of one device take every pair of d < 4 and r < 2 once.
All inputs are finite; a program needn't handle non-finite values.
Results may differ from a plain program's by a relative error of at most 0.0003.
Values sent between devices are 32-bit elements; how exact they have to be, the bound alone decides.
No kernel may reach another device: no remote copies, remote signals or barrier semaphores. Data moves between devices by JAX's collectives and lax.ppermute only.
A program may use at most 128 MiB of HBM per device.

v0:
```python
from functools import partial
import jax
import jax.numpy as jnp
from jax import lax
from jax.sharding import PartitionSpec as P

HIGH = lax.Precision.HIGHEST
NORM_EPS = 1e-05


def entering(x, axis, combine, identity, reverse):
    count, place = (lax.axis_size(axis), lax.axis_index(axis))
    everything = jax.tree.map(lambda part: lax.all_gather(part, axis), x)
    start = jax.tree.map(
        lambda part, zero: jnp.broadcast_to(jnp.asarray(zero, part.dtype), part.shape), x, identity
    )

    def lap(k, before):
        at = count - 1 - k if reverse else k
        reached = at > place if reverse else at < place
        new = combine(before, jax.tree.map(lambda part: part[at], everything))
        return jax.tree.map(lambda a, b: jnp.where(reached, a, b), new, before)

    return lax.fori_loop(0, count, lap, start)


def layer_norm(values, gain, shift):
    middle = jnp.mean(values, axis=-1, keepdims=True)
    centred = values - middle
    spread = jnp.mean(centred * centred, axis=-1, keepdims=True)
    return centred * lax.rsqrt(spread + NORM_EPS) * gain + shift


def feature_map(heads, weight):
    logits = jnp.einsum("rhd,hde->rhe", heads, weight, precision=HIGH)
    return jnp.concatenate(
        [jax.nn.softmax(logits, axis=-1), jax.nn.softmax(-logits, axis=-1)], axis=-1
    )


def segment_of(places, ends, total, number):
    found = jnp.sum((ends[None, :] <= places[:, None]).astype(jnp.int32), axis=1)
    found = jnp.where(places < 0, -1, found)
    return jnp.where(places >= total, number + 1, found)


def project(normed, weight, bias):
    return jnp.einsum("rd,dke->rke", normed, weight, precision=HIGH) + bias


def mlp_part(normed, up_full, up_bias, down_full):
    active = jax.nn.gelu(jnp.dot(normed, up_full, precision=HIGH) + up_bias, approximate=True)
    return jnp.dot(active, down_full, precision=HIGH)


def chain_join(earlier, later):
    passing = 1.0 - later[2]
    return (
        later[0] + passing * earlier[0],
        later[1] + passing * earlier[1],
        jnp.maximum(earlier[2], later[2]),
    )


def local_part(queries, keys, values, weight_q, weight_k, segment, seg_first, block):
    phi_q = feature_map(queries, weight_q)
    phi_k = feature_map(keys, weight_k)
    count_rows, local_heads, head_dim = values.shape
    feats = phi_q.shape[2]
    blocks = count_rows // block
    lower = jnp.arange(block)[:, None] >= jnp.arange(block)[None, :]

    def block_step(carry, pieces):
        state, normer, seg_carry = carry
        piece_q, piece_k, piece_v, seg_piece = pieces
        allowed = jnp.logical_and(lower, seg_piece[:, None] == seg_piece[None, :]).astype(
            jnp.float32
        )
        scores = jnp.einsum("ihf,jhf->hij", piece_q, piece_k, precision=HIGH) * allowed[None]
        numer = jnp.einsum("hij,jhd->ihd", scores, piece_v, precision=HIGH)
        denom = jnp.einsum("hij->ih", scores)
        carried = (seg_piece == seg_carry).astype(jnp.float32)
        numer = numer + carried[:, None, None] * jnp.einsum(
            "ihf,hfd->ihd", piece_q, state, precision=HIGH
        )
        denom = denom + carried[:, None] * jnp.einsum("ihf,hf->ih", piece_q, normer, precision=HIGH)
        final_seg = seg_piece[-1]
        stays = (final_seg == seg_carry).astype(jnp.float32)
        tail_k = piece_k * (seg_piece == final_seg).astype(jnp.float32)[:, None, None]
        state = stays * state + jnp.einsum("jhf,jhd->hfd", tail_k, piece_v, precision=HIGH)
        normer = stays * normer + jnp.sum(tail_k, axis=0)
        return ((state, normer, final_seg), (numer, denom))

    def blocked(array):
        return array.reshape((blocks, block) + array.shape[1:])

    start = (
        jnp.zeros((local_heads, feats, head_dim), jnp.float32),
        jnp.zeros((local_heads, feats), jnp.float32),
        seg_first,
    )
    (state, normer, _), (numer, denom) = lax.scan(
        jax.checkpoint(block_step),
        start,
        (blocked(phi_q), blocked(phi_k), blocked(values), blocked(segment)),
    )
    return (
        phi_q,
        numer.reshape(count_rows, local_heads, head_dim),
        denom.reshape(count_rows, local_heads),
        state,
        normer,
    )


def body(
    block_input,
    ln1_gain,
    ln1_shift,
    qkv_weight,
    qkv_bias,
    feat_query,
    feat_key,
    out_weight,
    out_bias,
    ln2_gain,
    ln2_shift,
    up_weight,
    up_bias,
    down_weight,
    down_bias,
    lengths,
    deal,
    cotangent,
):
    count_rows, width = block_input.shape
    local_heads, head_dim = (feat_query.shape[0], feat_query.shape[1])
    local_width = local_heads * head_dim
    offset = lax.axis_index(("fsdp", "context")) * count_rows
    total = count_rows * lax.axis_size(("fsdp", "context"))
    ends = jnp.cumsum(lengths)
    used = ends[-1]
    number = lengths.shape[0]
    places = offset + jnp.arange(count_rows, dtype=jnp.int32)
    segment = segment_of(places, ends, total, number)
    edges = segment_of(offset + jnp.array([-1, count_rows], dtype=jnp.int32), ends, total, number)
    seg_first = segment[0]
    seg_final = segment[-1]
    carry_in = (edges[0] == seg_first).astype(jnp.float32)
    breaks = (edges[0] != seg_final).astype(jnp.float32)
    valid = (places < used).astype(jnp.float32)[:, None]
    block = min(512, count_rows)
    qkv_full, out_full, up_full, down_full = (
        lax.all_gather(qkv_weight, ("fsdp", "context"), axis=0, tiled=True),
        lax.all_gather(out_weight, ("fsdp", "context"), axis=1, tiled=True),
        lax.all_gather(up_weight, ("fsdp", "context"), axis=0, tiled=True),
        lax.all_gather(down_weight, ("fsdp", "context"), axis=1, tiled=True),
    )
    normed1 = layer_norm(block_input, ln1_gain, ln1_shift)
    qkv = project(normed1, qkv_full, qkv_bias)
    queries = qkv[:, 0, :].reshape(count_rows, local_heads, head_dim)
    keys = qkv[:, 1, :].reshape(count_rows, local_heads, head_dim)
    values = qkv[:, 2, :].reshape(count_rows, local_heads, head_dim)
    attend_local = partial(local_part, segment=segment, seg_first=seg_first, block=block)
    phi_q, numer_local, denom_local, state_tail, norm_tail = attend_local(
        queries, keys, values, feat_query, feat_key
    )
    identity = (jnp.zeros_like(state_tail), jnp.zeros_like(norm_tail), jnp.zeros((), jnp.float32))
    state_scan, norm_scan, _ = entering(
        (state_tail, norm_tail, breaks), ("fsdp", "context"), chain_join, identity, False
    )
    state_in = carry_in * state_scan
    norm_in = carry_in * norm_scan
    first_rows = (segment == seg_first).astype(jnp.float32)[:, None, None]
    masked_q = phi_q * first_rows
    numer = numer_local + jnp.einsum("rhf,hfd->rhd", masked_q, state_in, precision=HIGH)
    denom = denom_local + jnp.einsum("rhf,hf->rh", masked_q, norm_in, precision=HIGH)
    attended = numer / denom[:, :, None]
    attended_flat = attended.reshape(count_rows, local_width)
    attn_part = jnp.dot(attended_flat, out_full, precision=HIGH)
    attn = lax.psum(attn_part, "tensor") + out_bias
    hidden = block_input + attn
    normed2 = layer_norm(hidden, ln2_gain, ln2_shift)
    slots = deal.shape[0]
    group_rows = count_rows // slots
    part_rows = group_rows // lax.axis_size("tensor")
    part_start = lax.axis_index("tensor") * part_rows
    per_peer = slots // lax.axis_size("context")
    slot_of = deal // slots % lax.axis_size("context") * per_peer + deal % per_peer
    counting = jnp.arange(slots, dtype=jnp.int32)
    source_of = jnp.sum(
        jnp.where(slot_of[None, :] == counting[:, None], counting[None, :], 0), axis=1
    )
    mlp_terms = mlp_part(normed2, up_full, up_bias, down_full)
    mlp = lax.psum(mlp_terms, "tensor") + down_bias
    result = hidden + mlp
    outbound = jnp.take(result.reshape(slots, group_rows, width), source_of, axis=0)
    dealt_whole = lax.all_to_all(outbound, "context", split_axis=0, concat_axis=0, tiled=True)
    dealt_output = lax.dynamic_slice_in_dim(dealt_whole, part_start, part_rows, 1)
    squares = jnp.stack(
        [jnp.sum(valid * result * result), jnp.sum(valid * attn * attn), jnp.sum(valid * mlp * mlp)]
    )
    inbound = lax.all_to_all(
        cotangent.reshape(slots, group_rows, width),
        "context",
        split_axis=0,
        concat_axis=0,
        tiled=True,
    )
    grad_y = jnp.take(inbound, slot_of, axis=0).reshape(count_rows, width) * valid
    grad_down_bias = jnp.sum(grad_y, axis=0)
    _, mlp_backward = jax.vjp(mlp_part, normed2, up_full, up_bias, down_full)
    grad_normed2_part, grad_up_full, grad_up_bias, grad_down_full = mlp_backward(grad_y)
    grad_normed2 = lax.psum(grad_normed2_part, "tensor")
    _, norm2_backward = jax.vjp(layer_norm, hidden, ln2_gain, ln2_shift)
    grad_hidden_norm, grad_ln2_gain, grad_ln2_shift = norm2_backward(grad_normed2)
    grad_hidden = grad_y + grad_hidden_norm
    grad_out_bias = jnp.sum(grad_hidden, axis=0)
    grad_out_full = jnp.einsum("rd,re->de", attended_flat, grad_hidden, precision=HIGH)
    grad_attended = jnp.einsum("re,de->rd", grad_hidden, out_full, precision=HIGH).reshape(
        count_rows, local_heads, head_dim
    )
    grad_numer = grad_attended / denom[:, :, None]
    grad_denom = -jnp.sum(grad_attended * attended, axis=2) / denom
    grad_state_in = carry_in * jnp.einsum("rhf,rhd->hfd", masked_q, grad_numer, precision=HIGH)
    grad_norm_in = carry_in * jnp.einsum("rhf,rh->hf", masked_q, grad_denom, precision=HIGH)
    grad_phi_extra = first_rows * (
        jnp.einsum("rhd,hfd->rhf", grad_numer, state_in, precision=HIGH)
        + grad_denom[:, :, None] * norm_in[None, :, :]
    )
    grad_state_tail, grad_norm_tail, _ = entering(
        (grad_state_in, grad_norm_in, breaks), ("fsdp", "context"), chain_join, identity, True
    )
    _, attention_backward = jax.vjp(attend_local, queries, keys, values, feat_query, feat_key)
    grad_queries, grad_keys, grad_values, grad_feat_query, grad_feat_key = attention_backward(
        (grad_phi_extra, grad_numer, grad_denom, grad_state_tail, grad_norm_tail)
    )
    grad_qkv = jnp.stack(
        [
            grad_queries.reshape(count_rows, local_width),
            grad_keys.reshape(count_rows, local_width),
            grad_values.reshape(count_rows, local_width),
        ],
        axis=1,
    )
    _, project_backward = jax.vjp(project, normed1, qkv_full, qkv_bias)
    grad_normed1_part, grad_qkv_full, grad_qkv_bias = project_backward(grad_qkv)
    grad_normed1 = lax.psum(grad_normed1_part, "tensor")
    _, norm1_backward = jax.vjp(layer_norm, block_input, ln1_gain, ln1_shift)
    grad_input_norm, grad_ln1_gain, grad_ln1_shift = norm1_backward(grad_normed1)
    grad_input = grad_hidden + grad_input_norm
    grad_qkv_weight, grad_out_weight, grad_up_weight, grad_down_weight = (
        lax.psum_scatter(grad_qkv_full, ("fsdp", "context"), scatter_dimension=0, tiled=True),
        lax.psum_scatter(grad_out_full, ("fsdp", "context"), scatter_dimension=1, tiled=True),
        lax.psum_scatter(grad_up_full, ("fsdp", "context"), scatter_dimension=0, tiled=True),
        lax.psum_scatter(grad_down_full, ("fsdp", "context"), scatter_dimension=1, tiled=True),
    )
    summed = lax.psum(
        (
            grad_ln1_gain,
            grad_ln1_shift,
            grad_qkv_bias,
            grad_feat_query,
            grad_feat_key,
            grad_out_bias,
            grad_ln2_gain,
            grad_ln2_shift,
            grad_up_bias,
            grad_down_bias,
            squares,
        ),
        ("fsdp", "context"),
    )
    rms = jnp.sqrt(summed[10] / (used.astype(jnp.float32) * width))
    return (
        dealt_output,
        rms,
        grad_input,
        summed[0],
        summed[1],
        grad_qkv_weight,
        summed[2],
        summed[3],
        summed[4],
        grad_out_weight,
        summed[5],
        summed[6],
        summed[7],
        grad_up_weight,
        summed[8],
        grad_down_weight,
        summed[9],
    )


def solution(mesh):
    in_specs = (
        P(("fsdp", "context"), None),
        P(),
        P(),
        P(("fsdp", "context"), None, "tensor"),
        P(None, "tensor"),
        P("tensor", None, None),
        P("tensor", None, None),
        P("tensor", ("fsdp", "context")),
        P(),
        P(),
        P(),
        P(("fsdp", "context"), "tensor"),
        P("tensor"),
        P("tensor", ("fsdp", "context")),
        P(),
        P(),
        P(("fsdp", "context")),
        P(("fsdp", "context"), None),
    )
    out_specs = (
        P(("fsdp", "context"), "tensor", None),
        P(),
        P(("fsdp", "context"), None),
        P(),
        P(),
        P(("fsdp", "context"), None, "tensor"),
        P(None, "tensor"),
        P("tensor", None, None),
        P("tensor", None, None),
        P("tensor", ("fsdp", "context")),
        P(),
        P(),
        P(),
        P(("fsdp", "context"), "tensor"),
        P("tensor"),
        P("tensor", ("fsdp", "context")),
        P(),
    )
    return jax.shard_map(body, mesh=mesh, in_specs=in_specs, out_specs=out_specs, check_vma=False)
```

profile of v0, /device:TPU:0, one launch (start us, length us, event | category | flops | bytes accessed | tf_op | source)
XLA Modules:
  0.0 1227.2 jit_solution(8723379923862665840)
XLA Ops:
  13.2 47.0 %all-gather.13.cloned.1.call-done = f32[768,3,384]{2,0,1:T(8,128)} async-done(((f32[48,3,384]{2,0,1:T(8,128)}), f32[768,3,384]{2,0,1:T(8,128)}) %all-gather.13.cloned.1.call-update) | async-done | bytes 3538960 | tf_op jit(solution)/shard_map/all_gather | solution.py:154
  82.2 43.4 %all-reduce = f32[16]{0:T(128)} all-reduce(f32[16]{0:T(128)S(1)} %dynamic-update-slice), channel_id=1, replica_groups=mesh['fsdp'=4,'context'=4,'tensor'=2] {'fsdp','context'}, use_global_device_ids=true, to_apply=%add | all-reduce | flops 16 | bytes 128
  130.5 31.8 %all-gather.4 = f32[16,6,128]{2,1,0:T(8,128)} all-gather(f32[1,6,128]{2,1,0:T(8,128)S(1)} %bitcast.196), channel_id=3, replica_groups=mesh['fsdp'=4,'context'=4,'tensor'=2] {'fsdp','context'}, dimensions={0}, use_global_device_ids=true | all-gather | bytes 52224 | tf_op jit(solution)/shard_map/all_gather | solution.py:13
  174.0 111.7 %while.22 = (s32[]{:T(128)}, f32[6,128,64]{2,1,0:T(8,128)}, f32[6,128]{1,0:T(8,128)}, s32[]{:T(128)}, f32[16,6,128,64]{2,3,1,0:T(8,128)}, /*index=5*/f32[16]{0:T...) while((s32[]{:T(128)}, f32[6,128,64]{2,1,0:T(8,128)}, f32[6,128]{1,0:T(8,128)}, ...), condition=%wide.region_15.16_spmd.clone, body=%wide.region_14.15_spmd.clone.sunk | while | flops 199685 | bytes 1385643 | solution.py:24
  310.1 33.8 %all-to-all-done.1 = f32[8,64,768]{2,1,0:T(8,128)S(1)} async-done(((f32[8,64,768]{2,1,0:T(8,128)}), f32[8,64,768]{2,1,0:T(8,128)S(1)}, u32[]{:S(2)}, u32[]{:S(2)}) %all-to-all-start.1) | async-done | bytes 1572896 | tf_op jit(solution)/shard_map/all_to_all | solution.py:203
  349.3 11.4 fusion.168
  362.8 47.3 %all-gather.17.cloned.1.call-done = f32[768,1536]{1,0:T(8,128)} async-done(((f32[48,1536]{1,0:T(8,128)}), f32[768,1536]{1,0:T(8,128)}) %all-gather.17.cloned.1.call-update) | async-done | bytes 4718608 | tf_op jit(solution)/shard_map/all_gather | solution.py:156
  410.1 14.9 %fusion.155 = (f32[1536]{0:T(1024)}, f32[512,1536]{1,0:T(8,128)S(1)}, f32[512,1536]{1,0:T(8,128)}) fusion(f32[512,1536]{1,0:T(8,128)} %fusion.168, f32[1536]{0:T(1024)S(1)} %copy-done.118, f32[768,1536]{1,0:T(8,128)} %all-gather.17.cloned.1.call-done, f32[512,768]{1,0:T(8,128)S(1)} %get-tuple-element.631, f32[768]{0:T(1024)S(1)} %copy-done.83, ...), kind=kOutput, calls=%fused_computation.257 | convolution fusion | flops 7265843712 | bytes 15751168 | tf_op jit(solution)/shard_map/dot_general | solution.py:52
  426.6 9.0 fusion.169
  435.9 50.0 %all-reduce.11.cloned.1.call-done = f32[512,768]{1,0:T(8,128)} async-done(((f32[512,768]{1,0:T(8,128)}), f32[512,768]{1,0:T(8,128)}) %all-reduce.11.cloned.1.call-update) | async-done | bytes 1572880 | tf_op jit(solution)/shard_map/psum | solution.py:214
  503.5 12.7 %fusion.38 = f32[512,768]{1,0:T(8,128)} fusion(f32[1536,768]{0,1:T(8,128)} %all-gather.19.cloned.1.call-done, f32[512,1536]{1,0:T(8,128)S(1)} %copy-done.124), kind=kOutput, calls=%fused_computation.80 | convolution fusion | flops 7254048768 | bytes 9437184 | tf_op jit(solution)/shard_map/dot_general | solution.py:53
  517.7 35.5 %all-gather.5 = f32[16,6,128]{2,1,0:T(8,128)} all-gather(f32[1,6,128]{2,1,0:T(8,128)S(1)} %fusion.126), channel_id=5, replica_groups=mesh['fsdp'=4,'context'=4,'tensor'=2] {'fsdp','context'}, dimensions={0}, use_global_device_ids=true | all-gather | bytes 52224 | tf_op jit(solution)/shard_map/all_gather | solution.py:13
  553.3 111.7 %while.23 = (s32[]{:T(128)}, f32[6,128,64]{2,1,0:T(8,128)}, f32[6,128]{1,0:T(8,128)}, s32[]{:T(128)}, f32[16,6,128,64]{2,3,1,0:T(8,128)}, /*index=5*/f32[16]{0:T...) while((s32[]{:T(128)}, f32[6,128,64]{2,1,0:T(8,128)}, ...), condition=%wide.region_31.33_spmd.clone, body=%wide.region_30.32_spmd.clone.sunk | while | flops 199689 | bytes 1385705 | solution.py:24
  688.9 8.5 fusion.13
  727.5 10.4 convolution_bitcast_fusion
  743.5 12.1 fusion.62
  755.6 12.1 fusion.37
  772.7 10.1 fusion.30
  783.6 37.0 %all-reduce.15.cloned.1.call-done = (f32[512,768]{1,0:T(8,128)}, f32[512,768]{1,0:T(8,128)}) async-done(((f32[512,768]{1,0:T(8,128)}, f32[512,768]{1,0:T(8,128)}), (f32[512,768]{1,0:T(8,128)}, f32[512,768]{1,0:T(8,128)})) %all-reduce.15.cloned.1.call-update) | async-done | bytes 3145744 | tf_op jit(solution)/shard_map/psum | solution.py:195
  837.8 89.3 %all-reduce.1 = (f32[3]{0:T(128)S(1)}, f32[768]{0:T(1024)}, f32[768]{0:T(1024)}, f32[3,384]{1,0:T(4,128)}, f32[768]{0:T(1024)}, /*index=5*/f32[768]{0:T(1024)}, f32[768]{0:T(1024)}, f32[1536]{0:T(1024)}, f32[768]{0:T(1024)}) all-reduce(f32[3]{0:T(128)S(1)} %pad_maximum_fusion.5, ...), channel_id=1, replica_groups=mesh['fsdp'=4,'context'=4,'tensor'=2] {'fsdp','context'}, use_global_device_ids=true, to_apply=%region_25.27 | all-reduce | flops 7299 | bytes 58392 | tf_op jit(solution)/shard_map/psum | solution.py:258
  932.4 38.8 %reduce-scatter.9.cloned.1.call-done = f32[48,1536]{1,0:T(8,128)} async-done(((f32[768,1536]{1,0:T(8,128)}), f32[48,1536]{1,0:T(8,128)}) %reduce-scatter.9.cloned.1.call-update) | async-done | bytes 294928 | tf_op jit(solution)/shard_map/reduce_scatter | solution.py:255
  971.2 79.1 %reduce-scatter.11.cloned.1.call-done = f32[1536,48]{0,1:T(8,128)} async-done(((f32[1536,768]{0,1:T(8,128)}), f32[1536,48]{0,1:T(8,128)}) %reduce-scatter.11.cloned.1.call-update) | async-done | bytes 294928 | tf_op jit(solution)/shard_map/reduce_scatter | solution.py:256
  1050.3 95.4 %all-reduce.13.cloned.1.call-done = (f32[6,64,64]{2,1,0:T(8,128)}, f32[6,64,64]{2,1,0:T(8,128)}) async-done(((f32[6,64,64]{2,1,0:T(8,128)}, f32[6,64,64]{2,1,0:T(8,128)}), (f32[6,64,64]{2,1,0:T(8,128)}, f32[6,64,64]{2,1,0:T(8,128)})) %all-reduce.13.cloned.1.call-update) | async-done | bytes 196624 | tf_op jit(solution)/shard_map/psum | solution.py:258
  1145.7 71.5 %reduce-scatter.5.cloned.1.call-done = f32[48,3,384]{2,0,1:T(8,128)} async-done(((f32[768,3,384]{2,0,1:T(8,128)}), f32[48,3,384]{2,0,1:T(8,128)}) %reduce-scatter.5.cloned.1.call-update) | async-done | bytes 221200 | tf_op jit(solution)/shard_map/reduce_scatter | solution.py:253
  (568 shorter events, 387.0 us)
Async XLA Ops:
  7.2 53.1 %all-gather.13.cloned.1.call-start = ((), (), s32[]{:S(2)}) async-start(), calls=%async_computation.6 | async-start | bytes 3760128 | tf_op jit(solution)/shard_map/all_gather | solution.py:154
  8.0 166.0 %all-gather.21.cloned.1.call-start = ((), (), s32[]{:S(2)}) async-start(), calls=%async_computation.16 | async-start | bytes 3342336 | tf_op jit(solution)/shard_map/all_gather | solution.py:13
  13.2 150.8 %copy-start.75 = (f32[512]{0:T(512)}, f32[512]{0:T(512)S(1)}, u32[]{:S(2)}) copy-start(f32[512]{0:T(512)S(1)} %get-tuple-element.642) | copy-start | bytes 6148
  72.0 429.7 %copy-start.58 = (f32[512,6]{0,1:T(8,128)}, f32[512,6]{0,1:T(8,128)S(1)}, u32[]{:S(2)}) copy-start(f32[512,6]{0,1:T(8,128)S(1)} %get-tuple-element.645) | copy-start | bytes 36868
  76.8 220.4 %all-gather.15.cloned.1.call-start = ((), (), s32[]{:S(2)}) async-start(), calls=%async_computation.7 | async-start | bytes 1253376 | tf_op jit(solution)/shard_map/all_gather | solution.py:155
  77.6 271.8 %all-gather.19.cloned.1.call-start = ((), (), s32[]{:S(2)}) async-start(), calls=%async_computation.10 | async-start | bytes 5013504 | tf_op jit(solution)/shard_map/all_gather | solution.py:157
  78.1 282.6 %all-reduce.9.cloned.1.call-start = ((), (), s32[]{:S(2)}) async-start(), calls=%async_computation.8 | async-start | bytes 3145728 | tf_op jit(solution)/shard_map/psum | solution.py:181
  162.6 126.7 %copy-start.2 = (f32[512,6,64]{0,2,1:T(8,128)}, f32[512,6,64]{0,2,1:T(8,128)S(1)}, u32[]{:S(2)}) copy-start(f32[512,6,64]{0,2,1:T(8,128)S(1)} %get-tuple-element.658) | copy-start | bytes 2359300
  162.6 126.7 %copy-start.5 = (f32[512,6,64]{0,2,1:T(8,128)}, f32[512,6,64]{0,2,1:T(8,128)S(1)}, u32[]{:S(2)}) copy-start(f32[512,6,64]{0,2,1:T(8,128)S(1)} %get-tuple-element.659) | copy-start | bytes 2359300
  303.8 106.3 %all-gather.17.cloned.1.call-start = ((), (), s32[]{:S(2)}) async-start(), calls=%async_computation.9 | async-start | bytes 5013504 | tf_op jit(solution)/shard_map/all_gather | solution.py:156
  304.4 39.4 %all-to-all-start.1 = ((f32[8,64,768]{2,1,0:T(8,128)}), f32[8,64,768]{2,1,0:T(8,128)S(1)}, u32[]{:S(2)}, u32[]{:S(2)}) async-start(f32[8,64,768]{2,1,0:T(8,128)} %bitcast.190), calls=%async_computation.1 | async-start | bytes 3145728 | tf_op jit(solution)/shard_map/all_to_all | solution.py:203
  308.0 177.9 %all-reduce.11.cloned.1.call-start = ((), (), s32[]{:S(2)}) async-start(), calls=%async_computation.11 | async-start | bytes 3145728 | tf_op jit(solution)/shard_map/psum | solution.py:214
  309.3 180.0 %copy-start.97 = (f32[512]{0:T(512)}, f32[512]{0:T(512)S(1)}, u32[]{:S(2)}) copy-start(f32[512]{0:T(512)S(1)} %fusion.132) | copy-start | bytes 6148
  362.5 126.2 %copy-start.81 = (f32[512]{0:T(512)}, f32[512]{0:T(512)S(1)}, u32[]{:S(2)}) copy-start(f32[512]{0:T(512)S(1)} %broadcast_multiply_fusion.1) | copy-start | bytes 6148
  362.8 125.9 %copy-start.90 = (f32[512]{0:T(512)}, f32[512]{0:T(512)S(1)}, u32[]{:S(2)}) copy-start(f32[512]{0:T(512)S(1)} %fusion.134) | copy-start | bytes 6148
  435.7 117.6 %all-gather.23.cloned.1.call-start = ((), (), s32[]{:S(2)}) async-start(), calls=%async_computation.17 | async-start | bytes 3342336 | tf_op jit(solution)/shard_map/all_gather | solution.py:13
  497.9 322.7 %all-reduce.15.cloned.1.call-start = ((), (), s32[]{:S(2)}) async-start(), calls=%async_computation.19 | async-start | bytes 6291456 | tf_op jit(solution)/shard_map/psum | solution.py:195
  737.9 194.5 %reduce-scatter.7.cloned.1.call-start = ((), (), s32[]{:S(2)}) async-start(), calls=%async_computation.13 | async-start | bytes 1253376 | tf_op jit(solution)/shard_map/reduce_scatter | solution.py:254
  743.4 227.8 %reduce-scatter.9.cloned.1.call-start = ((), (), s32[]{:S(2)}) async-start(), calls=%async_computation.14 | async-start | bytes 5013504 | tf_op jit(solution)/shard_map/reduce_scatter | solution.py:255
  755.6 294.7 %reduce-scatter.11.cloned.1.call-start = ((), (), s32[]{:S(2)}) async-start(), calls=%async_computation.15 | async-start | bytes 5013504 | tf_op jit(solution)/shard_map/reduce_scatter | solution.py:256
  767.8 377.9 %all-reduce.13.cloned.1.call-start = ((), (), s32[]{:S(2)}) async-start(), calls=%async_computation.18 | async-start | bytes 786432 | tf_op jit(solution)/shard_map/psum | solution.py:258
  772.4 444.8 %reduce-scatter.5.cloned.1.call-start = ((), (), s32[]{:S(2)}) async-start(), calls=%async_computation.12 | async-start | bytes 3760128 | tf_op jit(solution)/shard_map/reduce_scatter | solution.py:253
  828.1 102.2 %all-to-all-start = ((f32[8,64,768]{2,1,0:T(8,128)}), f32[8,64,768]{2,1,0:T(8,128)}, u32[]{:S(2)}, u32[]{:S(2)}) async-start(f32[8,64,768]{2,1,0:T(8,128)} %broadcast_select_fusion.1), calls=%async_computation | async-start | bytes 3145728 | tf_op jit(solution)/shard_map/all_to_all | solution.py:198
  837.0 90.5 %copy-start.49 = (f32[512,768]{1,0:T(8,128)S(1)}, f32[512,768]{1,0:T(8,128)}, u32[]{:S(2)}) copy-start(f32[512,768]{1,0:T(8,128)} %get-tuple-element.616) | copy-start | bytes 4718596
  (117 other events, 1409.7 us)
Sparse Core Ops, SparseCore 0:
  10.4 49.8 all-gather.12
  76.9 44.2 all-gather.20
  123.5 36.9 all-gather.14
  162.7 51.7 all-gather.18
  304.0 50.9 all-reduce.8
  357.1 52.9 all-gather.16
  435.8 50.0 all-reduce.10
  498.0 45.7 all-gather.22
  738.0 82.5 all-reduce.14
  824.7 67.4 reduce-scatter.6
  896.6 74.5 reduce-scatter.8
  975.5 74.7 reduce-scatter.10
  1054.9 90.7 all-reduce.12
  1150.0 67.1 reduce-scatter.4
where the time goes:
time: 1240 us; the launch traced here: 1230 us
  waiting for transfers between devices  503 us (41%)
  blocking collectives  200 us (16%)
  matrix products  192 us (15%)
  other arithmetic  149 us (12%)
  local copies, waits for them, and re-layouts  136 us (11%)
  loops' own time  21.4 us (2%)
  between operations  17.7 us (1%)
    select_n x64, other arithmetic, lap(): return jax.tree.map(lambda a, b: jnp.where(reached, a, b), new, before)  103 us
    dynamic_slice x96, local copies, waits for them, and re-layouts, lap(): new = combine(before, jax.tree.map(lambda part: part[at], everything))  99.5 us
    psum x1, waiting for transfers between devices, body(): lax.psum((grad_ln1_gain, grad_ln1_shift, grad_qkv_bias, grad_feat_query,...  95.4 us
    psum x1, blocking collectives, body(): lax.psum((grad_ln1_gain, grad_ln1_shift, grad_qkv_bias, grad_feat_query,...  89.3 us
    reduce_scatter x1, waiting for transfers between devices, body(): lax.psum_scatter(grad_down_full, ('fsdp', 'context'), scatter_dimension=1...  79.1 us
    reduce_scatter x1, waiting for transfers between devices, body(): lax.psum_scatter(grad_qkv_full, ('fsdp', 'context'), scatter_dimension=0,...  71.5 us
    all_gather x2, blocking collectives, entering(): everything = jax.tree.map(lambda part: lax.all_gather(part, axis), x)  67.3 us
    psum x1, waiting for transfers between devices, body(): grad_normed2 = lax.psum(grad_normed2_part, 'tensor')  50 us
  transfers between devices with their start and end apart: 16, of which 9 were waited for; matrix products, arithmetic and copies ran while one was open for 20% of the time, Pallas kernels for 0%

commit v1 on v0

--- a/solution.py
+++ b/solution.py
@@ -1,3 +1,4 @@
+import functools
 from functools import partial
 import jax
 import jax.numpy as jnp
@@ -6,6 +7,31 @@
 
 HIGH = lax.Precision.HIGHEST
 NORM_EPS = 1e-05
+
+
+def search_the_racks(frame_in, dim_no, work_x):
+    ready, piece_out = (frame_in.shape[:dim_no], frame_in.shape[dim_no + 1 :])
+    return jnp.moveaxis(frame_in.reshape(*ready, work_x, -1, *piece_out), dim_no, 0)
+
+
+def rest_sections(field, k_dim):
+    small = list(field.shape[1:])
+    small[k_dim] *= field.shape[0]
+    return jnp.moveaxis(field, 0, k_dim).reshape(small)
+
+
+def zones_hold(inp, mesh_name, v0, sample):
+    arr_next, g_now = (lax.axis_size(mesh_name), lax.axis_index(mesh_name))
+    f_next = search_the_racks(inp, v0, arr_next)
+    buffer = [f_next[g_now]]
+    for m in range(1, arr_next):
+        oldest = f_next[g_now ^ m]
+        buffer.append(lax.ppermute(oldest, mesh_name, perm=[(c, c ^ m) for c in range(arr_next)]))
+    f_next = jnp.stack(buffer, 0)[g_now ^ jnp.arange(arr_next)]
+    return rest_sections(f_next, sample)
+
+
+obtain_the_view = functools.partial(zones_hold, mesh_name="context", v0=0, sample=0)
 
 
 def entering(x, axis, combine, identity, reverse):
@@ -200,13 +226,7 @@
     squares = jnp.stack(
         [jnp.sum(valid * result * result), jnp.sum(valid * attn * attn), jnp.sum(valid * mlp * mlp)]
     )
-    inbound = lax.all_to_all(
-        cotangent.reshape(slots, group_rows, width),
-        "context",
-        split_axis=0,
-        concat_axis=0,
-        tiled=True,
-    )
+    inbound = obtain_the_view(cotangent.reshape(slots, group_rows, width))
     grad_y = jnp.take(inbound, slot_of, axis=0).reshape(count_rows, width) * valid
     grad_down_bias = jnp.sum(grad_y, axis=0)
     _, mlp_backward = jax.vjp(mlp_part, normed2, up_full, up_bias, down_full)

time: 1240 us -> 1240 us (level)
    all_to_all x1 -> x0, waiting for transfers between devices: 33.8 us -> none  [body(): lax.all_to_all(cotangent.reshape(slots, group_rows, width), 'context', sp...]
    ppermute x0 -> x3, waiting for transfers between devices: none -> 27.5 us  [zones_hold(): lax.ppermute(oldest, mesh_name, perm=[(c, c ^ m) for c in range(arr_next)])]
  transfers between devices with their start and end apart: 16 -> 18, of which waited for: 9 -> 10; matrix products, arithmetic and copies ran while one was open for 20% -> 20% of each run, Pallas kernels for 0% -> 0%
where the time goes in v1:
time: 1240 us; the launch traced here: 1230 us
  waiting for transfers between devices  500 us (40%)
  blocking collectives  199 us (16%)
  matrix products  192 us (15%)
  other arithmetic  148 us (12%)
  local copies, waits for them, and re-layouts  139 us (11%)
  loops' own time  21.4 us (2%)
  between operations  17.8 us (1%)
    select_n x64, other arithmetic, lap(): return jax.tree.map(lambda a, b: jnp.where(reached, a, b), new, before)  103 us
    dynamic_slice x96, local copies, waits for them, and re-layouts, lap(): new = combine(before, jax.tree.map(lambda part: part[at], everything))  100 us
    psum x1, waiting for transfers between devices, body(): lax.psum((grad_ln1_gain, grad_ln1_shift, grad_qkv_bias, grad_feat_query,...  95.4 us
    psum x1, blocking collectives, body(): lax.psum((grad_ln1_gain, grad_ln1_shift, grad_qkv_bias, grad_feat_query,...  89.2 us
    reduce_scatter x1, waiting for transfers between devices, body(): lax.psum_scatter(grad_down_full, ('fsdp', 'context'), scatter_dimension=1...  79.1 us
    reduce_scatter x1, waiting for transfers between devices, body(): lax.psum_scatter(grad_qkv_full, ('fsdp', 'context'), scatter_dimension=0,...  71.5 us
    all_gather x2, blocking collectives, entering(): everything = jax.tree.map(lambda part: lax.all_gather(part, axis), x)  67.3 us
    all_gather x1, waiting for transfers between devices, body(): lax.all_gather(up_weight, ('fsdp', 'context'), axis=0, tiled=True)  51 us
  transfers between devices with their start and end apart: 18, of which 10 were waited for; matrix products, arithmetic and copies ran while one was open for 20% of the time, Pallas kernels for 0%

profile of v1, /device:TPU:0, one launch (start us, length us, event | category | flops | bytes accessed | tf_op | source)
XLA Modules:
  0.0 1227.6 jit_solution(2083504591726448617)
XLA Ops:
  13.3 47.0 %all-gather.13.cloned.1.call-done = f32[768,3,384]{2,0,1:T(8,128)} async-done(((f32[48,3,384]{2,0,1:T(8,128)}), f32[768,3,384]{2,0,1:T(8,128)}) %all-gather.13.cloned.1.call-update) | async-done | bytes 3538960 | tf_op jit(solution)/shard_map/all_gather | solution.py:180
  82.3 42.9 %all-reduce = f32[16]{0:T(128)} all-reduce(f32[16]{0:T(128)S(1)} %dynamic-update-slice), channel_id=1, replica_groups=mesh['fsdp'=4,'context'=4,'tensor'=2] {'fsdp','context'}, use_global_device_ids=true, to_apply=%add | all-reduce | flops 16 | bytes 128
  130.1 31.8 %all-gather.4 = f32[16,6,128]{2,1,0:T(8,128)} all-gather(f32[1,6,128]{2,1,0:T(8,128)S(1)} %bitcast.212), channel_id=3, replica_groups=mesh['fsdp'=4,'context'=4,'tensor'=2] {'fsdp','context'}, dimensions={0}, use_global_device_ids=true | all-gather | bytes 52224 | tf_op jit(solution)/shard_map/all_gather | solution.py:39
  173.5 112.2 %while.22 = (s32[]{:T(128)}, f32[6,128,64]{2,1,0:T(8,128)}, f32[6,128]{1,0:T(8,128)}, s32[]{:T(128)}, f32[16,6,128,64]{2,3,1,0:T(8,128)}, /*index=5*/f32[16]{0:T...) while((s32[]{:T(128)}, f32[6,128,64]{2,1,0:T(8,128)}, f32[6,128]{1,0:T(8,128)}, ...), condition=%wide.region_15.16_spmd.clone, body=%wide.region_14.15_spmd.clone.sunk | while | flops 199685 | bytes 1385643 | solution.py:50
  319.3 20.0 %collective-permute-done.1 = f32[2,64,768]{2,1,0:T(8,128)S(1)} collective-permute-done((f32[2,64,768]{2,1,0:T(8,128)S(1)}, f32[2,64,768]{2,1,0:T(8,128)S(1)}, u32[]{:S(2)}, u32[]{:S(2)}) %collective-permute-start.1) | collective-permute-done | bytes 393248 | tf_op jit(solution)/shard_map/ppermute | solution.py:29
  345.6 11.4 fusion.169
  359.1 51.0 %all-gather.17.cloned.1.call-done = f32[768,1536]{1,0:T(8,128)} async-done(((f32[48,1536]{1,0:T(8,128)}), f32[768,1536]{1,0:T(8,128)}) %all-gather.17.cloned.1.call-update) | async-done | bytes 4718608 | tf_op jit(solution)/shard_map/all_gather | solution.py:182
  410.1 14.9 %fusion.156 = (f32[1536]{0:T(1024)}, f32[512,1536]{1,0:T(8,128)S(1)}, f32[512,1536]{1,0:T(8,128)}) fusion(f32[512,1536]{1,0:T(8,128)} %fusion.169, f32[1536]{0:T(1024)S(1)} %copy-done.119, f32[768,1536]{1,0:T(8,128)} %all-gather.17.cloned.1.call-done, f32[512,768]{1,0:T(8,128)S(1)} %get-tuple-element.631, f32[768]{0:T(1024)S(1)} %copy-done.84, ...), kind=kOutput, calls=%fused_computation.266 | convolution fusion | flops 7265843712 | bytes 15751168 | tf_op jit(solution)/shard_map/dot_general | solution.py:78
  426.6 9.1 fusion.170
  435.9 50.0 %all-reduce.11.cloned.1.call-done = f32[512,768]{1,0:T(8,128)} async-done(((f32[512,768]{1,0:T(8,128)}), f32[512,768]{1,0:T(8,128)}) %all-reduce.11.cloned.1.call-update) | async-done | bytes 1572880 | tf_op jit(solution)/shard_map/psum | solution.py:234
  503.5 12.7 %fusion.38 = f32[512,768]{1,0:T(8,128)} fusion(f32[1536,768]{0,1:T(8,128)} %all-gather.19.cloned.1.call-done, f32[512,1536]{1,0:T(8,128)S(1)} %copy-done.125), kind=kOutput, calls=%fused_computation.82 | convolution fusion | flops 7254048768 | bytes 9437184 | tf_op jit(solution)/shard_map/dot_general | solution.py:79
  517.7 35.5 %all-gather.5 = f32[16,6,128]{2,1,0:T(8,128)} all-gather(f32[1,6,128]{2,1,0:T(8,128)S(1)} %fusion.126), channel_id=5, replica_groups=mesh['fsdp'=4,'context'=4,'tensor'=2] {'fsdp','context'}, dimensions={0}, use_global_device_ids=true | all-gather | bytes 52224 | tf_op jit(solution)/shard_map/all_gather | solution.py:39
  553.3 112.1 %while.23 = (s32[]{:T(128)}, f32[6,128,64]{2,1,0:T(8,128)}, f32[6,128]{1,0:T(8,128)}, s32[]{:T(128)}, f32[16,6,128,64]{2,3,1,0:T(8,128)}, /*index=5*/f32[16]{0:T...) while((s32[]{:T(128)}, f32[6,128,64]{2,1,0:T(8,128)}, ...), condition=%wide.region_31.33_spmd.clone, body=%wide.region_30.32_spmd.clone.sunk | while | flops 199689 | bytes 1385705 | solution.py:50
  689.3 8.5 fusion.13
  728.0 10.4 convolution_bitcast_fusion
  744.0 12.1 fusion.62
  756.2 12.1 fusion.37
  773.2 10.1 fusion.30
  784.2 37.0 %all-reduce.15.cloned.1.call-done = (f32[512,768]{1,0:T(8,128)}, f32[512,768]{1,0:T(8,128)}) async-done(((f32[512,768]{1,0:T(8,128)}, f32[512,768]{1,0:T(8,128)}), (f32[512,768]{1,0:T(8,128)}, f32[512,768]{1,0:T(8,128)})) %all-reduce.15.cloned.1.call-update) | async-done | bytes 3145744 | tf_op jit(solution)/shard_map/psum | solution.py:221
  838.3 89.2 %all-reduce.1 = (f32[3]{0:T(128)S(1)}, f32[768]{0:T(1024)}, f32[768]{0:T(1024)}, f32[3,384]{1,0:T(4,128)}, f32[768]{0:T(1024)}, /*index=5*/f32[768]{0:T(1024)}, f32[768]{0:T(1024)}, f32[1536]{0:T(1024)}, f32[768]{0:T(1024)}) all-reduce(f32[3]{0:T(128)S(1)} %pad_maximum_fusion.6, ...), channel_id=1, replica_groups=mesh['fsdp'=4,'context'=4,'tensor'=2] {'fsdp','context'}, use_global_device_ids=true, to_apply=%region_25.27 | all-reduce | flops 7299 | bytes 58392 | tf_op jit(solution)/shard_map/psum | solution.py:278
  932.9 38.8 %reduce-scatter.9.cloned.1.call-done = f32[48,1536]{1,0:T(8,128)} async-done(((f32[768,1536]{1,0:T(8,128)}), f32[48,1536]{1,0:T(8,128)}) %reduce-scatter.9.cloned.1.call-update) | async-done | bytes 294928 | tf_op jit(solution)/shard_map/reduce_scatter | solution.py:275
  971.7 79.1 %reduce-scatter.11.cloned.1.call-done = f32[1536,48]{0,1:T(8,128)} async-done(((f32[1536,768]{0,1:T(8,128)}), f32[1536,48]{0,1:T(8,128)}) %reduce-scatter.11.cloned.1.call-update) | async-done | bytes 294928 | tf_op jit(solution)/shard_map/reduce_scatter | solution.py:276
  1050.8 95.4 %all-reduce.13.cloned.1.call-done = (f32[6,64,64]{2,1,0:T(8,128)}, f32[6,64,64]{2,1,0:T(8,128)}) async-done(((f32[6,64,64]{2,1,0:T(8,128)}, f32[6,64,64]{2,1,0:T(8,128)}), (f32[6,64,64]{2,1,0:T(8,128)}, f32[6,64,64]{2,1,0:T(8,128)})) %all-reduce.13.cloned.1.call-update) | async-done | bytes 196624 | tf_op jit(solution)/shard_map/psum | solution.py:278
  1146.2 71.5 %reduce-scatter.5.cloned.1.call-done = f32[48,3,384]{2,0,1:T(8,128)} async-done(((f32[768,3,384]{2,0,1:T(8,128)}), f32[48,3,384]{2,0,1:T(8,128)}) %reduce-scatter.5.cloned.1.call-update) | async-done | bytes 221200 | tf_op jit(solution)/shard_map/reduce_scatter | solution.py:273
  (579 shorter events, 398.0 us)
Async XLA Ops:
  7.2 53.1 %all-gather.13.cloned.1.call-start = ((), (), s32[]{:S(2)}) async-start(), calls=%async_computation.5 | async-start | bytes 3760128 | tf_op jit(solution)/shard_map/all_gather | solution.py:180
  8.0 165.6 %all-gather.21.cloned.1.call-start = ((), (), s32[]{:S(2)}) async-start(), calls=%async_computation.15 | async-start | bytes 3342336 | tf_op jit(solution)/shard_map/all_gather | solution.py:39
  13.3 150.3 %copy-start.76 = (f32[512]{0:T(512)}, f32[512]{0:T(512)S(1)}, u32[]{:S(2)}) copy-start(f32[512]{0:T(512)S(1)} %get-tuple-element.646) | copy-start | bytes 6148
  72.0 429.7 %copy-start.59 = (f32[512,6]{0,1:T(8,128)}, f32[512,6]{0,1:T(8,128)S(1)}, u32[]{:S(2)}) copy-start(f32[512,6]{0,1:T(8,128)S(1)} %get-tuple-element.649) | copy-start | bytes 36868
  76.8 220.4 %all-gather.15.cloned.1.call-start = ((), (), s32[]{:S(2)}) async-start(), calls=%async_computation.6 | async-start | bytes 1253376 | tf_op jit(solution)/shard_map/all_gather | solution.py:181
  77.6 268.0 %all-gather.19.cloned.1.call-start = ((), (), s32[]{:S(2)}) async-start(), calls=%async_computation.9 | async-start | bytes 5013504 | tf_op jit(solution)/shard_map/all_gather | solution.py:183
  78.1 278.9 %all-reduce.9.cloned.1.call-start = ((), (), s32[]{:S(2)}) async-start(), calls=%async_computation.7 | async-start | bytes 3145728 | tf_op jit(solution)/shard_map/psum | solution.py:207
  162.1 127.2 %copy-start.2 = (f32[512,6,64]{0,2,1:T(8,128)}, f32[512,6,64]{0,2,1:T(8,128)S(1)}, u32[]{:S(2)}) copy-start(f32[512,6,64]{0,2,1:T(8,128)S(1)} %get-tuple-element.662) | copy-start | bytes 2359300
  303.9 106.2 %all-gather.17.cloned.1.call-start = ((), (), s32[]{:S(2)}) async-start(), calls=%async_computation.8 | async-start | bytes 5013504 | tf_op jit(solution)/shard_map/all_gather | solution.py:182
  304.4 181.5 %all-reduce.11.cloned.1.call-start = ((), (), s32[]{:S(2)}) async-start(), calls=%async_computation.10 | async-start | bytes 3145728 | tf_op jit(solution)/shard_map/psum | solution.py:234
  305.4 13.9 %collective-permute-start.2 = (f32[2,64,768]{2,1,0:T(8,128)S(1)}, f32[2,64,768]{2,1,0:T(8,128)S(1)}, u32[]{:S(2)}, u32[]{:S(2)}) collective-permute-start(f32[2,64,768]{2,1,0:T(8,128)S(1)} %get-tuple-element.636), channel_id=1, source_target_pairs={{0,6},{2,4},{4,2},{6,0},{1,7},{3,5},{5,3},{7,1},{8,14},{10,12},{12... | collective-permute-start | bytes 1179656 | tf_op jit(solution)/shard_map/ppermute | solution.py:29
  306.4 32.9 %collective-permute-start.1 = (f32[2,64,768]{2,1,0:T(8,128)S(1)}, f32[2,64,768]{2,1,0:T(8,128)S(1)}, u32[]{:S(2)}, u32[]{:S(2)}) collective-permute-start(f32[2,64,768]{2,1,0:T(8,128)S(1)} %get-tuple-element.637), channel_id=1, source_target_pairs={{0,4},{2,6},{4,0},{6,2},{1,5},{3,7},{5,1},{7,3},{8,12},{10,14},{12... | collective-permute-start | bytes 1179656 | tf_op jit(solution)/shard_map/ppermute | solution.py:29
  308.6 30.7 %collective-permute-start = (f32[2,64,768]{2,1,0:T(8,128)S(1)}, f32[2,64,768]{2,1,0:T(8,128)S(1)}, u32[]{:S(2)}, u32[]{:S(2)}) collective-permute-start(f32[2,64,768]{2,1,0:T(8,128)S(1)} %get-tuple-element.638), channel_id=1, source_target_pairs={{0,2},{2,0},{4,6},{6,4},{1,3},{3,1},{5,7},{7,5},{8,10},{10,8},{12,... | collective-permute-start | bytes 1179656 | tf_op jit(solution)/shard_map/ppermute | solution.py:29
  311.8 177.6 %copy-start.98 = (f32[512]{0:T(512)}, f32[512]{0:T(512)S(1)}, u32[]{:S(2)}) copy-start(f32[512]{0:T(512)S(1)} %fusion.132) | copy-start | bytes 6148
  358.7 129.9 %copy-start.82 = (f32[512]{0:T(512)}, f32[512]{0:T(512)S(1)}, u32[]{:S(2)}) copy-start(f32[512]{0:T(512)S(1)} %broadcast_multiply_fusion.1) | copy-start | bytes 6148
  359.1 129.6 %copy-start.91 = (f32[512]{0:T(512)}, f32[512]{0:T(512)S(1)}, u32[]{:S(2)}) copy-start(f32[512]{0:T(512)S(1)} %fusion.134) | copy-start | bytes 6148
  435.7 117.6 %all-gather.23.cloned.1.call-start = ((), (), s32[]{:S(2)}) async-start(), calls=%async_computation.16 | async-start | bytes 3342336 | tf_op jit(solution)/shard_map/all_gather | solution.py:39
  497.9 323.2 %all-reduce.15.cloned.1.call-start = ((), (), s32[]{:S(2)}) async-start(), calls=%async_computation.18 | async-start | bytes 6291456 | tf_op jit(solution)/shard_map/psum | solution.py:221
  738.5 194.4 %reduce-scatter.7.cloned.1.call-start = ((), (), s32[]{:S(2)}) async-start(), calls=%async_computation.12 | async-start | bytes 1253376 | tf_op jit(solution)/shard_map/reduce_scatter | solution.py:274
  743.9 227.8 %reduce-scatter.9.cloned.1.call-start = ((), (), s32[]{:S(2)}) async-start(), calls=%async_computation.13 | async-start | bytes 5013504 | tf_op jit(solution)/shard_map/reduce_scatter | solution.py:275
  756.1 294.7 %reduce-scatter.11.cloned.1.call-start = ((), (), s32[]{:S(2)}) async-start(), calls=%async_computation.14 | async-start | bytes 5013504 | tf_op jit(solution)/shard_map/reduce_scatter | solution.py:276
  768.3 377.9 %all-reduce.13.cloned.1.call-start = ((), (), s32[]{:S(2)}) async-start(), calls=%async_computation.17 | async-start | bytes 786432 | tf_op jit(solution)/shard_map/psum | solution.py:278
  773.0 444.7 %reduce-scatter.5.cloned.1.call-start = ((), (), s32[]{:S(2)}) async-start(), calls=%async_computation.11 | async-start | bytes 3760128 | tf_op jit(solution)/shard_map/reduce_scatter | solution.py:273
  828.6 102.2 %all-to-all-start = ((f32[8,64,768]{2,1,0:T(8,128)}), f32[8,64,768]{2,1,0:T(8,128)}, u32[]{:S(2)}, u32[]{:S(2)}) async-start(f32[8,64,768]{2,1,0:T(8,128)} %broadcast_select_fusion.1), calls=%async_computation | async-start | bytes 3145728 | tf_op jit(solution)/shard_map/all_to_all | solution.py:224
  (120 other events, 1605.4 us)
Sparse Core Ops, SparseCore 0:
  10.4 49.8 all-gather.12
  77.0 44.1 all-gather.20
  123.5 36.9 all-gather.14
  162.6 51.8 all-gather.18
  304.0 50.9 all-reduce.8
  357.1 52.9 all-gather.16
  435.8 50.0 all-reduce.10
  498.0 45.6 all-gather.22
  738.5 82.5 all-reduce.14
  825.2 67.4 reduce-scatter.6
  897.1 74.5 reduce-scatter.8
  976.0 74.7 reduce-scatter.10
  1055.4 90.7 all-reduce.12
  1150.5 67.1 reduce-scatter.4
